TPU v7x, 32 devices: a whole 2x2x4 slice. The times are simulated.
32 devices in a mesh: groups: 2 (over x), segment: 4 (over y, core), head: 4 (over z).
Axes of the slice: x: 2, y: 2, z: 4, core: 2. Of those that a mesh axis runs over, the one named last changes fastest.
Arguments:
- token_ids: int32 [6, 256], P('groups'), parts along dimension 0, may hold values from 0 to 18991, as said below
- embed_table: bfloat16 [18992, 256], P(('segment', 'head')), may hold values from -6 to 6
- arriving: bfloat16 [8, 256, 256], P(('groups', 'segment')), parts along dimension 0, may hold values from -16 to 16
- returning: bfloat16 [8, 256, 256], P(('groups', 'segment')), parts along dimension 0, may hold values from -6 to 6
- stashed: bfloat16 [8, 3, 256, 256], P(('groups', 'segment')), parts along dimension 0, may hold values from -16 to 16
- seed_grad: bfloat16 [6, 256, 256], P('groups'), parts along dimension 0, may hold values from -6 to 6
- expand: bfloat16 [4, 256, 2048], P('segment'), may hold values from -0.375 to 0.375
- compress: bfloat16 [4, 2048, 256], P('segment'), may hold values from -0.125 to 0.125
- norm_gain: float32 [4, 2048], P('segment'), may hold values from 0.1 to 1.9
- w_query: bfloat16 [4, 2048, 4096], P('segment', None, 'head'), may hold values from -0.125 to 0.125
- key_weight: bfloat16 [4, 2048, 512], P('segment'), may hold values from -0.125 to 0.125
- value_weight: bfloat16 [4, 2048, 512], P('segment'), may hold values from -0.125 to 0.125
- w_out: bfloat16 [4, 4096, 2048], P('segment', 'head'), may hold values from -0.09375 to 0.09375
Outputs:
- sent_forward: bfloat16 [8, 3, 256, 256], P(('groups', 'segment'), None, 'head'), parts along dimension 0
- sent_backward: bfloat16 [8, 3, 256, 256], P(('groups', 'segment'), None, 'head'), parts along dimension 0
There are 2 independent parts, one for each index of `groups`. A program takes and returns all parts, laid end to end along the dimension named above; an argument that names none is the same for every part. Nothing has to cross between parts.
Inputs may be any that keep to these rules, and one draw needn't show every extreme that they name: `token_ids`: every aligned block of 1187 ids is named by some token.
All inputs are finite; a program needn't handle non-finite values.
Results may differ from a plain program's by a relative error of at most 0.02.
Values may be sent and summed in bfloat16 or wider, within the bound.
A program may use at most 128 MiB of HBM per device.

v0:
```python
import math

import jax
import jax.numpy as jnp
from jax import lax
from jax.sharding import PartitionSpec as P

QUERY_HEADS = 32
KEY_VALUE_HEADS = 4
HEAD_SIZE = 128


EPS = 1e-06


def passed_along(x, axis, by):
    length = lax.axis_size(axis)
    pairs = [(i, i + by) for i in range(length) if 0 <= i + by < length]
    return lax.ppermute(x, axis, pairs)


def rms_scale(matrix):
    return lax.rsqrt(jnp.mean(matrix * matrix, axis=-1, keepdims=True) + EPS)


def precise(former, latter):
    return jnp.dot(
        former, latter, precision=lax.Precision.HIGHEST, preferred_element_type=jnp.float32
    )


def precise_back(former, latter):
    return lax.dot_general(
        former,
        latter,
        (((1,), (1,)), ((), ())),
        precision=lax.Precision.HIGHEST,
        preferred_element_type=jnp.float32,
    )


def narrow_back(former, latter):
    return lax.dot_general(
        former, latter, (((1,), (1,)), ((), ())), preferred_element_type=jnp.float32
    )


def norm_back(upstream_in, grad_hat):
    scaling = rms_scale(upstream_in)
    return scaling * grad_hat - upstream_in * scaling**3 * jnp.mean(
        grad_hat * upstream_in, axis=-1, keepdims=True
    )


def section_inputs(coeffs, expand_here, gain_here, query_here, key_here, value_here):
    row_count = coeffs.shape[0]
    hidden = jnp.dot(coeffs, expand_here, preferred_element_type=jnp.float32)
    scaling = rms_scale(hidden)
    normed = (hidden * scaling * gain_here).astype(jnp.bfloat16)
    queries = jnp.dot(normed, query_here, preferred_element_type=jnp.float32).reshape(
        row_count, -1, HEAD_SIZE
    )
    key_rows = jnp.dot(normed, key_here, preferred_element_type=jnp.float32).reshape(
        row_count, -1, HEAD_SIZE
    )
    values = (
        jnp.dot(normed, value_here, preferred_element_type=jnp.float32)
        .astype(jnp.bfloat16)
        .reshape(row_count, -1, HEAD_SIZE)
    )
    q_hat = (queries * rms_scale(queries)).astype(jnp.bfloat16)
    k_hat = (key_rows * rms_scale(key_rows)).astype(jnp.bfloat16)
    return (hidden, scaling, queries, key_rows, q_hat, k_hat, values)


def probabilities(q_hat, k_hat):
    row_count, head_count, head_width = q_hat.shape
    kv_heads = k_hat.shape[1]
    grouped = q_hat.reshape(row_count, kv_heads, head_count // kv_heads, head_width)
    scores = jnp.einsum(
        "iknd,jkd->knij", grouped, k_hat, preferred_element_type=jnp.float32
    ) / math.sqrt(head_width)
    causal = jnp.arange(row_count)[None, :] <= jnp.arange(row_count)[:, None]
    weights = jnp.where(causal, jnp.exp(scores), 0.0)
    return weights / jnp.sum(weights, axis=-1, keepdims=True)


def section_forward(coeffs, expand_here, gain_here, query_here, key_here, value_here, out_folded):
    hidden, scaling, queries, key_rows, q_hat, k_hat, values = section_inputs(
        coeffs, expand_here, gain_here, query_here, key_here, value_here
    )
    weights = probabilities(q_hat, k_hat)
    attended = jnp.einsum(
        "knij,jkd->iknd", weights.astype(jnp.bfloat16), values, preferred_element_type=jnp.float32
    )
    attended = attended.reshape(coeffs.shape[0], -1).astype(jnp.bfloat16)
    return jnp.dot(attended, out_folded, preferred_element_type=jnp.float32)


def section_backward(
    coeffs, grads, expand_here, gain_here, query_here, key_here, value_here, out_folded
):
    row_count = coeffs.shape[0]
    hidden, scaling, queries, key_rows, q_hat, k_hat, values = section_inputs(
        coeffs, expand_here, gain_here, query_here, key_here, value_here
    )
    weights = probabilities(q_hat, k_hat)
    head_count = queries.shape[1]
    kv_heads = key_rows.shape[1]
    query_group_size = head_count // kv_heads
    grad_attended = narrow_back(grads, out_folded).astype(jnp.bfloat16)
    grad_attended = grad_attended.reshape(row_count, kv_heads, query_group_size, HEAD_SIZE)
    grad_weights = jnp.einsum(
        "iknd,jkd->knij", grad_attended, values, preferred_element_type=jnp.float32
    )
    grad_scores = (
        weights
        * (grad_weights - jnp.sum(grad_weights * weights, axis=-1, keepdims=True))
        / math.sqrt(HEAD_SIZE)
    )
    grad_scores = grad_scores.astype(jnp.bfloat16)
    grouped = q_hat.reshape(row_count, kv_heads, query_group_size, HEAD_SIZE)
    grad_qhat = jnp.einsum(
        "knij,jkd->iknd", grad_scores, k_hat, preferred_element_type=jnp.float32
    ).reshape(row_count, head_count, HEAD_SIZE)
    grad_khat = jnp.einsum(
        "knij,iknd->jkd", grad_scores, grouped, preferred_element_type=jnp.float32
    )
    grad_values = jnp.einsum(
        "knij,iknd->jkd",
        weights.astype(jnp.bfloat16),
        grad_attended,
        preferred_element_type=jnp.float32,
    )
    grad_values = grad_values.reshape(row_count, -1).astype(jnp.bfloat16)
    grad_queries = norm_back(queries, grad_qhat).reshape(row_count, -1).astype(jnp.bfloat16)
    grad_keys = norm_back(key_rows, grad_khat).reshape(row_count, -1).astype(jnp.bfloat16)
    grad_normed = (
        narrow_back(grad_queries, query_here)
        + narrow_back(grad_keys, key_here)
        + narrow_back(grad_values, value_here)
    )
    weighted = grad_normed * gain_here
    grad_hidden = scaling * weighted - hidden * scaling**3 * jnp.mean(
        weighted * hidden, axis=-1, keepdims=True
    )
    return narrow_back(grad_hidden.astype(jnp.bfloat16), expand_here)


def shards(
    token_ids,
    embed_table,
    arriving,
    returning,
    stashed,
    seed_grad,
    expand,
    compress,
    norm_gain,
    w_query,
    key_weight,
    value_weight,
    w_out,
):
    segment_index = lax.axis_index("segment")
    last_segment = lax.axis_size("segment") - 1
    head_index = lax.axis_index("head")
    heads_here = w_query.shape[2] // HEAD_SIZE
    query_group_size = QUERY_HEADS // KEY_VALUE_HEADS
    kv_here = (heads_here + query_group_size - 1) // query_group_size
    first_kv = head_index * heads_here // query_group_size
    expand_here = expand[0]
    gain_here = norm_gain[0]
    query_here = w_query[0]
    key_here = lax.dynamic_slice_in_dim(key_weight[0], first_kv * HEAD_SIZE, kv_here * HEAD_SIZE, 1)
    value_here = lax.dynamic_slice_in_dim(
        value_weight[0], first_kv * HEAD_SIZE, kv_here * HEAD_SIZE, 1
    )
    basis_folded = jnp.dot(expand_here, compress[0], preferred_element_type=jnp.float32)
    out_folded = jnp.dot(w_out[0], compress[0], preferred_element_type=jnp.float32).astype(
        jnp.bfloat16
    )
    table_rows = embed_table.shape[0]
    local_ids = token_ids.reshape(-1) - lax.axis_index(("segment", "head")) * table_rows
    inside = (local_ids >= 0) & (local_ids < table_rows)
    looked = jnp.take(embed_table, jnp.clip(local_ids, 0, table_rows - 1), axis=0).astype(
        jnp.float32
    )
    picked = jnp.where(inside[:, None], looked, 0.0)
    embedded = lax.psum(picked, ("segment", "head")).astype(jnp.bfloat16)
    tick_count = token_ids.shape[0]
    span_rows = token_ids.shape[1]
    embedded = embedded.reshape(tick_count, span_rows, -1)
    share_rows = span_rows // lax.axis_size("head")
    share_start = head_index * share_rows
    forward_recv = arriving[0]
    backward_recv = returning[0]
    history = []
    forward_shares = []
    backward_shares = []
    for tick_index in range(tick_count):
        more_ticks = tick_index + 1 < tick_count
        forward_in = jnp.where(segment_index == 0, embedded[tick_index], forward_recv)
        backward_in = jnp.where(segment_index == last_segment, seed_grad[tick_index], backward_recv)
        history.append(forward_in)
        delay_ticks = 2 * (last_segment - segment_index)
        replay = stashed[0, tick_index]
        for earlier in range(tick_index + 1):
            replay = jnp.where(delay_ticks == tick_index - earlier, history[earlier], replay)
        partial_value = section_forward(
            forward_in, expand_here, gain_here, query_here, key_here, value_here, out_folded
        )
        direct = precise(forward_in.astype(jnp.float32), basis_folded)
        summed = lax.psum_scatter(
            partial_value.astype(jnp.bfloat16), "head", scatter_dimension=0, tiled=True
        ).astype(jnp.float32)
        own_rows = (summed + lax.dynamic_slice_in_dim(direct, share_start, share_rows, 0)).astype(
            jnp.bfloat16
        )
        forward_shares.append(own_rows)
        if more_ticks:
            arrived = passed_along(own_rows, "segment", 1)
            forward_recv = lax.all_gather(arrived, "head", axis=0, tiled=True)
        partial_back = section_backward(
            replay,
            backward_in,
            expand_here,
            gain_here,
            query_here,
            key_here,
            value_here,
            out_folded,
        )
        direct_back = precise_back(backward_in.astype(jnp.float32), basis_folded)
        summed_back = lax.psum_scatter(
            partial_back.astype(jnp.bfloat16), "head", scatter_dimension=0, tiled=True
        ).astype(jnp.float32)
        own_back = (
            summed_back + lax.dynamic_slice_in_dim(direct_back, share_start, share_rows, 0)
        ).astype(jnp.bfloat16)
        backward_shares.append(own_back)
        if more_ticks:
            arrived_back = passed_along(own_back, "segment", -1)
            backward_recv = lax.all_gather(arrived_back, "head", axis=0, tiled=True)
    sent_forward = jnp.stack(forward_shares)[None]
    sent_backward = jnp.stack(backward_shares)[None]
    return (sent_forward, sent_backward)


def solution(mesh):
    return jax.shard_map(
        shards,
        mesh=mesh,
        in_specs=(
            P("groups", None),
            P(("segment", "head"), None),
            P(("groups", "segment"), None, None),
            P(("groups", "segment"), None, None),
            P(("groups", "segment"), None, None, None),
            P("groups", None, None),
            P("segment", None, None),
            P("segment", None, None),
            P("segment", None),
            P("segment", None, "head"),
            P("segment", None, None),
            P("segment", None, None),
            P("segment", "head", None),
        ),
        out_specs=(
            P(("groups", "segment"), None, "head", None),
            P(("groups", "segment"), None, "head", None),
        ),
        check_vma=False,
    )
```

profile of v0, /device:TPU:0, one launch (start us, length us, event | category | flops | bytes accessed | tf_op | source)
XLA Modules:
  0.0 454.9 jit_solution(9600917615611538147)
XLA Ops:
  9.6 4.0 gather_fusion
  15.9 78.0 %all-reduce.1 = bf16[768,256]{1,0:T(8,128)(2,1)} all-reduce(f32[768,256]{1,0:T(8,128)} %convert_select_fusion), channel_id=1, replica_groups=mesh['groups'=2,'segment'=4,'head'=4] {'segment','head'}, use_global_device_ids=true, to_apply=%region_0.1 | all-reduce | flops 196608 | bytes 1179648 | tf_op jit(solution)/shard_map/psum | solution.py:190
  101.1 6.5 %copy.87 = bf16[1024,2048]{1,0:T(8,128)(2,1)} copy(bf16[1024,2048]{0,1:T(8,128)(2,1)} %bitcast.659) | data formatting | bytes 8388608 | tf_op jit(solution)/shard_map/dot_general | solution.py:60
  107.6 3.9 multiply_reduce_fusion.17
  115.7 3.7 convolution_convert_fusion.5
  131.3 9.0 %reduce-scatter.7.cloned.1.call-done = bf16[64,256]{1,0:T(8,128)(2,1)} async-done(((bf16[256,256]{1,0:T(8,128)(2,1)}), bf16[64,256]{1,0:T(8,128)(2,1)}) %reduce-scatter.7.cloned.1.call-update) | async-done | bytes 32784 | tf_op jit(solution)/shard_map/reduce_scatter | solution.py:214
  146.1 14.0 %all_gather.12 = bf16[256,256]{1,0:T(8,128)(2,1)S(1)} all-gather(bf16[64,256]{1,0:T(8,128)(2,1)} %collective-permute-done), channel_id=1, replica_groups=mesh['groups'=2,'segment'=4,'head'=4] {'head'}, dimensions={0}, use_global_device_ids=true | all-gather | bytes 163840 | tf_op jit(solution)/shard_map/all_gather | solution.py:223
  179.7 3.8 convolution_convert_fusion.4
  192.4 12.4 %reduce-scatter.9.cloned.1.call-done = bf16[64,256]{1,0:T(8,128)(2,1)} async-done(((bf16[256,256]{1,0:T(8,128)(2,1)}), bf16[64,256]{1,0:T(8,128)(2,1)}) %reduce-scatter.9.cloned.1.call-update) | async-done | bytes 32784 | tf_op jit(solution)/shard_map/reduce_scatter | solution.py:214
  208.7 14.1 %all_gather.13 = bf16[256,256]{1,0:T(8,128)(2,1)S(1)} all-gather(bf16[64,256]{1,0:T(8,128)(2,1)S(1)} %collective-permute-done.1), channel_id=1, replica_groups=mesh['groups'=2,'segment'=4,'head'=4] {'head'}, dimensions={0}, use_global_device_ids=true | all-gather | bytes 163840 | tf_op jit(solution)/shard_map/all_gather | solution.py:223
  232.7 3.3 fusion.31
  235.9 5.0 %fusion.19 = (f32[8,256]{1,0:T(8,128)}, f32[256,256,8]{1,0,2:T(8,128)}) fusion(f32[8,256]{1,0:T(8,128)S(1)} %get-tuple-element.5, f32[256,256,8]{1,0,2:T(8,128)} %fusion.141, pred[256,256]{0,1:T(8,128)(4,1)S(1)} %copy-done.28, bf16[256,2048]{1,0:T(8,128)(2,1)} %copy-done.13, bf16[1,2048,512]{2,1,0:T(8,128)(2,1)S(1)} %copy-done, s32[]{:T(128)S(6)} %select_n.142, ...), kind=kOutput, calls=%fused_computation.38 | convolution fusion | flops 271087616 | bytes 6373380 | tf_op jit(solution)/shard_map/iknd,jkd->knij/dot_general | solution.py:113
  240.9 4.1 convert_bitcast_fusion.2
  257.5 3.6 fusion.4
  264.0 5.1 %multiply_reduce_fusion.4 = (f32[256]{0:T(256)S(1)}, f32[256,2048]{1,0:T(8,128)}) fusion(f32[256,2048]{1,0:T(8,128)} %get-tuple-element.49, f32[2048]{0:T(1024)S(1)} %bitcast.678, f32[256,2048]{1,0:T(8,128)} %convolution_add_fusion.5, bf16[1,2048,512]{2,1,0:T(8,128)(2,1)S(1)} %copy-done, s32[]{:T(128)S(6)} %select_n.142, ...), kind=kOutput, calls=%fused_computation.51 | convolution fusion | flops 270565120 | bytes 8397828 | tf_op jit(solution)/shard_map/dot_general | solution.py:43
  269.1 3.5 convolution_convert_fusion.11
  276.3 16.1 %reduce-scatter.13.cloned.1.call-done = bf16[64,256]{1,0:T(8,128)(2,1)} async-done(((bf16[256,256]{1,0:T(8,128)(2,1)}), bf16[64,256]{1,0:T(8,128)(2,1)}) %reduce-scatter.13.cloned.1.call-update) | async-done | bytes 32784 | tf_op jit(solution)/shard_map/reduce_scatter | solution.py:235
  296.4 13.6 %all_gather.14 = bf16[256,256]{1,0:T(8,128)(2,1)S(1)} all-gather(bf16[64,256]{1,0:T(8,128)(2,1)S(1)} %collective-permute-done.2), channel_id=1, replica_groups=mesh['groups'=2,'segment'=4,'head'=4] {'head'}, dimensions={0}, use_global_device_ids=true | all-gather | bytes 163840 | tf_op jit(solution)/shard_map/all_gather | solution.py:244
  312.8 5.0 %fusion.15 = (f32[8,256]{1,0:T(8,128)}, f32[256,256,8]{1,0,2:T(8,128)}) fusion(f32[8,256]{1,0:T(8,128)} %get-tuple-element.6, f32[256,256,8]{1,0,2:T(8,128)} %copy-done.10, pred[256,256]{0,1:T(8,128)(4,1)S(1)} %copy-done.29, bf16[256,2048]{1,0:T(8,128)(2,1)} %copy-done.12, bf16[1,2048,512]{2,1,0:T(8,128)(2,1)S(1)} %copy-done, s32[]{:T(128)S(6)} %select_n.142, ...), kind=kOutput, calls=%fused_computation.32 | convolution fusion | flops 271087616 | bytes 6373380 | tf_op jit(solution)/shard_map/iknd,jkd->knij/dot_general | solution.py:113
  317.8 4.0 convert_bitcast_fusion.1
  332.1 3.6 fusion.2
  338.5 5.1 %multiply_reduce_fusion.2 = (f32[256]{0:T(256)S(1)}, f32[256,2048]{1,0:T(8,128)}) fusion(f32[256,2048]{1,0:T(8,128)} %copy-done.3, f32[2048]{0:T(1024)S(1)} %bitcast.679, f32[256,2048]{1,0:T(8,128)} %convolution_add_fusion.3, bf16[1,2048,512]{2,1,0:T(8,128)(2,1)S(1)} %copy-done, s32[]{:T(128)S(6)} %select_n.142, bf16[256,8,128]{2,1,0:T(8,128)(2,1)} %bitcast.671, ...), kind=kOutput, calls=%fused_computation.47 | convolution fusion | flops 270565120 | bytes 8397828 | tf_op jit(solution)/shard_map/dot_general | solution.py:43
  343.6 3.5 convolution_convert_fusion.10
  352.3 12.9 %reduce-scatter.15.cloned.1.call-done = bf16[64,256]{1,0:T(8,128)(2,1)} async-done(((bf16[256,256]{1,0:T(8,128)(2,1)}), bf16[64,256]{1,0:T(8,128)(2,1)}) %reduce-scatter.15.cloned.1.call-update) | async-done | bytes 32784 | tf_op jit(solution)/shard_map/reduce_scatter | solution.py:235
  369.5 13.5 %all_gather.15 = bf16[256,256]{1,0:T(8,128)(2,1)S(1)} all-gather(bf16[64,256]{1,0:T(8,128)(2,1)S(1)} %collective-permute-done.3), channel_id=1, replica_groups=mesh['groups'=2,'segment'=4,'head'=4] {'head'}, dimensions={0}, use_global_device_ids=true | all-gather | bytes 163840 | tf_op jit(solution)/shard_map/all_gather | solution.py:244
  385.9 5.4 %fusion.11 = (f32[8,256]{1,0:T(8,128)S(1)}, f32[8,256]{1,0:T(8,128)S(1)}, f32[256,256,8]{1,0,2:T(8,128)}) fusion(f32[8,256]{1,0:T(8,128)S(1)} %copy-done.68, f32[256,256,8]{1,0,2:T(8,128)} %get-tuple-element.76, pred[256,256]{0,1:T(8,128)(4,1)S(1)} %copy-done.30, f32[256,256,8]{1,0,2:T(8,128)} %fusion.101, bf16[256,2048]{1,0:T(8,128)(2,1)} %copy-done.20, ...), kind=kOutput, calls=%fused_computation.26 | convolution fusion | flops 272658432 | bytes 8478724 | tf_op jit(solution)/shard_map/iknd,jkd->knij/dot_general | solution.py:113
  391.3 4.0 convert_bitcast_fusion
  398.7 3.8 convolution_convert_fusion.3
  409.2 3.6 fusion.6
  415.7 5.1 %multiply_reduce_fusion = (f32[256]{0:T(256)S(1)}, f32[256,2048]{1,0:T(8,128)}) fusion(f32[256,2048]{1,0:T(8,128)} %copy-done.2, f32[2048]{0:T(1024)S(1)} %bitcast.680, f32[256,2048]{1,0:T(8,128)} %convolution_add_fusion.1, bf16[1,2048,512]{2,1,0:T(8,128)(2,1)S(1)} %copy-done, s32[]{:T(128)S(6)} %select_n.142, bf16[256,8,128]{2,1,0:T(8,128)(2,1)} %bitcast.670, ...), kind=kOutput, calls=%fused_computation.43 | convolution fusion | flops 270565120 | bytes 8397828 | tf_op jit(solution)/shard_map/dot_general | solution.py:43
  420.8 3.5 convolution_convert_fusion.9
  428.2 17.5 %reduce-scatter.17.cloned.1.call-done = bf16[64,256]{1,0:T(8,128)(2,1)} async-done(((bf16[256,256]{1,0:T(8,128)(2,1)}), bf16[64,256]{1,0:T(8,128)(2,1)}) %reduce-scatter.17.cloned.1.call-update) | async-done | bytes 32784 | tf_op jit(solution)/shard_map/reduce_scatter | solution.py:235
  (282 shorter events, 145.8 us)
Async XLA Ops:
  7.2 108.5 %copy-start = (bf16[1,2048,512]{2,1,0:T(8,128)(2,1)S(1)}, bf16[1,2048,512]{2,1,0:T(8,128)(2,1)}, u32[]{:S(2)}) copy-start(bf16[1,2048,512]{2,1,0:T(8,128)(2,1)} %param.24) | copy-start | bytes 6291460
  7.2 133.1 %reduce-scatter.7.cloned.1.call-start = ((), (), s32[]{:S(2)}) async-start(), calls=%async_computation.6 | async-start | bytes 163840 | tf_op jit(solution)/shard_map/reduce_scatter | solution.py:214
  9.5 106.2 %copy-start.26 = (pred[256,256]{0,1:T(8,128)(4,1)}, pred[256,256]{0,1:T(8,128)(4,1)S(1)}, u32[]{:S(2)}) copy-start(pred[256,256]{0,1:T(8,128)(4,1)S(1)} %iota_compare_fusion) | copy-start | bytes 196612
  9.6 84.3 %copy-start.49 = (bf16[1,256,256]{2,1,0:T(8,128)(2,1)S(1)}, bf16[1,256,256]{2,1,0:T(8,128)(2,1)}, u32[]{:S(2)}) copy-start(bf16[1,256,256]{2,1,0:T(8,128)(2,1)} %param.15) | copy-start | bytes 393220
  13.6 81.3 %copy-start.1 = (bf16[1,256,2048]{2,1,0:T(8,128)(2,1)S(1)}, bf16[1,256,2048]{2,1,0:T(8,128)(2,1)}, u32[]{:S(2)}) copy-start(bf16[1,256,2048]{2,1,0:T(8,128)(2,1)} %param.19) | copy-start | bytes 3145732
  121.6 83.1 %reduce-scatter.9.cloned.1.call-start = ((), (), s32[]{:S(2)}) async-start(), calls=%async_computation.7 | async-start | bytes 163840 | tf_op jit(solution)/shard_map/reduce_scatter | solution.py:214
  141.8 4.4 collective-permute-start
  144.2 19.6 %copy-start.66 = (f32[256]{0:T(256)}, f32[256]{0:T(256)S(1)}, u32[]{:S(2)}) copy-start(f32[256]{0:T(256)S(1)} %get-tuple-element.33) | copy-start | bytes 3076
  164.5 5.7 %copy-start.12 = (bf16[256,2048]{1,0:T(8,128)(2,1)}, bf16[256,2048]{1,0:T(8,128)(2,1)S(1)}, u32[]{:S(2)}) copy-start(bf16[256,2048]{1,0:T(8,128)(2,1)S(1)} %get-tuple-element.19) | copy-start | bytes 3145732
  164.5 6.2 %copy-start.14 = (bf16[256,2048]{1,0:T(8,128)(2,1)}, bf16[256,2048]{1,0:T(8,128)(2,1)S(1)}, u32[]{:S(2)}) copy-start(bf16[256,2048]{1,0:T(8,128)(2,1)S(1)} %get-tuple-element.20) | copy-start | bytes 3145732
  164.5 8.6 %copy-start.13 = (bf16[256,2048]{1,0:T(8,128)(2,1)}, bf16[256,2048]{1,0:T(8,128)(2,1)S(1)}, u32[]{:S(2)}) copy-start(bf16[256,2048]{1,0:T(8,128)(2,1)S(1)} %get-tuple-element.21) | copy-start | bytes 3145732
  185.7 106.7 %reduce-scatter.13.cloned.1.call-start = ((), (), s32[]{:S(2)}) async-start(), calls=%async_computation.9 | async-start | bytes 163840 | tf_op jit(solution)/shard_map/reduce_scatter | solution.py:235
  185.8 5.0 %copy-start.71 = (f32[256]{0:T(256)S(1)}, f32[256]{0:T(256)}, u32[]{:S(2)}) copy-start(f32[256]{0:T(256)} %get-tuple-element.74) | copy-start | bytes 3076
  185.8 5.6 %copy-start.22 = (bf16[256,256]{1,0:T(8,128)(2,1)S(1)}, bf16[256,256]{1,0:T(8,128)(2,1)}, u32[]{:S(2)}) copy-start(bf16[256,256]{1,0:T(8,128)(2,1)} %copy-done.21) | copy-start | bytes 393220
  205.6 3.1 collective-permute-start.1
  208.7 24.0 %copy-start.10 = (f32[256,256,8]{1,0,2:T(8,128)}, f32[256,256,8]{1,0,2:T(8,128)S(1)}, u32[]{:S(2)}) copy-start(f32[256,256,8]{1,0,2:T(8,128)S(1)} %fusion.142) | copy-start | bytes 6291460
  208.7 15.6 %copy-start.23 = (bf16[256,256]{1,0:T(8,128)(2,1)S(1)}, bf16[256,256]{1,0:T(8,128)(2,1)}, u32[]{:S(2)}) copy-start(bf16[256,256]{1,0:T(8,128)(2,1)} %copy-done.21) | copy-start | bytes 393220
  235.9 5.0 %copy-start.69 = (f32[8,256]{1,0:T(8,128)}, f32[8,256]{1,0:T(8,128)S(1)}, u32[]{:S(2)}) copy-start(f32[8,256]{1,0:T(8,128)S(1)} %get-tuple-element.5) | copy-start | bytes 24580
  264.0 5.1 %copy-start.67 = (f32[256]{0:T(256)S(1)}, f32[256]{0:T(256)}, u32[]{:S(2)}) copy-start(f32[256]{0:T(256)} %copy-done.66) | copy-start | bytes 3076
  264.0 5.1 %copy-start.74 = (f32[256]{0:T(256)S(1)}, f32[256]{0:T(256)}, u32[]{:S(2)}) copy-start(f32[256]{0:T(256)} %get-tuple-element.32) | copy-start | bytes 3076
  272.6 40.3 %copy-start.29 = (pred[256,256]{0,1:T(8,128)(4,1)S(1)}, pred[256,256]{0,1:T(8,128)(4,1)}, u32[]{:S(2)}) copy-start(pred[256,256]{0,1:T(8,128)(4,1)} %copy-done.26) | copy-start | bytes 196612
  272.6 92.6 %reduce-scatter.15.cloned.1.call-start = ((), (), s32[]{:S(2)}) async-start(), calls=%async_computation.10 | async-start | bytes 163840 | tf_op jit(solution)/shard_map/reduce_scatter | solution.py:235
  293.2 24.6 %copy-start.51 = (bf16[64,256]{1,0:T(8,128)(2,1)}, bf16[64,256]{1,0:T(8,128)(2,1)S(1)}, u32[]{:S(2)}) copy-start(bf16[64,256]{1,0:T(8,128)(2,1)S(1)} %add_convert_fusion.2) | copy-start | bytes 98308
  293.3 3.1 collective-permute-start.2
  347.2 78.7 %reduce-scatter.11.cloned.1.call-start = ((), (), s32[]{:S(2)}) async-start(), calls=%async_computation.8 | async-start | bytes 163840 | tf_op jit(solution)/shard_map/reduce_scatter | solution.py:214
  350.2 35.6 %copy-start.30 = (pred[256,256]{0,1:T(8,128)(4,1)S(1)}, pred[256,256]{0,1:T(8,128)(4,1)}, u32[]{:S(2)}) copy-start(pred[256,256]{0,1:T(8,128)(4,1)} %copy-done.26) | copy-start | bytes 196612
  350.3 35.6 %copy-start.68 = (f32[8,256]{1,0:T(8,128)S(1)}, f32[8,256]{1,0:T(8,128)}, u32[]{:S(2)}) copy-start(f32[8,256]{1,0:T(8,128)} %get-tuple-element.4) | copy-start | bytes 24580
  366.0 25.3 %copy-start.52 = (bf16[64,256]{1,0:T(8,128)(2,1)}, bf16[64,256]{1,0:T(8,128)(2,1)S(1)}, u32[]{:S(2)}) copy-start(bf16[64,256]{1,0:T(8,128)(2,1)S(1)} %add_convert_fusion.1) | copy-start | bytes 98308
  366.0 3.4 collective-permute-start.3
  407.4 38.3 %reduce-scatter.17.cloned.1.call-start = ((), (), s32[]{:S(2)}) async-start(), calls=%async_computation.11 | async-start | bytes 163840 | tf_op jit(solution)/shard_map/reduce_scatter | solution.py:235
  415.7 5.1 %copy-start.62 = (f32[256]{0:T(256)S(1)}, f32[256]{0:T(256)}, u32[]{:S(2)}) copy-start(f32[256]{0:T(256)} %copy-done.61) | copy-start | bytes 3076
  415.7 5.1 %copy-start.72 = (f32[256]{0:T(256)S(1)}, f32[256]{0:T(256)}, u32[]{:S(2)}) copy-start(f32[256]{0:T(256)} %get-tuple-element.24) | copy-start | bytes 3076
  (56 other events, 165.4 us)
Sparse Core Ops, SparseCore 0:
  121.7 18.5 reduce-scatter.6
  185.8 18.8 reduce-scatter.8
  272.7 19.6 reduce-scatter.12
  347.3 17.8 reduce-scatter.14
  407.5 18.3 reduce-scatter.10
  428.0 17.6 reduce-scatter.16
where the time goes:
time: 463 us; the launch traced here: 455 us
  matrix products  156 us (34%)
  blocking collectives  133 us (29%)
  waiting for transfers between devices  68.8 us (15%)
  other arithmetic  47.6 us (10%)
  local copies, waits for them, and re-layouts  27.6 us (6%)
  between operations  15.2 us (3%)
  starting transfers between devices  6.22 us (1%)
    psum x1, blocking collectives, shards(): embedded = lax.psum(picked, ('segment', 'head')).astype(jnp.bfloat16)  78 us
    dot_general x15, matrix products, narrow_back(): lax.dot_general(former, latter, (((1,), (1,)), ((), ())), preferred_eleme...  51.8 us
    reduce_scatter x3, waiting for transfers between devices, shards(): lax.psum_scatter(partial_back.astype(jnp.bfloat16), 'head', scatter_dimen...  46.5 us
    all_gather x2, blocking collectives, shards(): forward_recv = lax.all_gather(arrived, 'head', axis=0, tiled=True)  28.1 us
    all_gather x2, blocking collectives, shards(): backward_recv = lax.all_gather(arrived_back, 'head', axis=0, tiled=True)  27.1 us
    reduce_scatter x3, waiting for transfers between devices, shards(): lax.psum_scatter(partial_value.astype(jnp.bfloat16), 'head', scatter_dime...  21.7 us
    dot_general x6, matrix products, probabilities(): jnp.einsum('iknd,jkd->knij', grouped, k_hat, preferred_element_type=jnp.f...  15.5 us
    dot_general x3, matrix products, section_backward(): jnp.einsum('iknd,jkd->knij', grad_attended, values, preferred_element_typ...  15.3 us
  transfers between devices with their start and end apart: 10, of which 7 were waited for; matrix products, arithmetic and copies ran while one was open for 11% of the time, Pallas kernels for 0%

commit v1 on v0

v1 whole, which is shorter than its diff:
```python
import functools
import math

import jax
import jax.numpy as jnp
from jax import lax
from jax.experimental import pallas as pl
from jax.experimental.pallas import tpu as pltpu
from jax.sharding import PartitionSpec as P

QUERY_HEADS = 32
KEY_VALUE_HEADS = 4
HEAD_SIZE = 128
EPS = 1e-06
MESH = pl.DeviceIdType.MESH
F32 = jnp.float32
BF16 = jnp.bfloat16


def mm(former, latter):
    return jnp.dot(former, latter, preferred_element_type=F32)


def mm_back(former, latter):
    return lax.dot_general(former, latter, (((1,), (1,)), ((), ())), preferred_element_type=F32)


def mm_down(former, latter):
    return lax.dot_general(former, latter, (((0,), (0,)), ((), ())), preferred_element_type=F32)


def halves(matrix):
    upper = matrix.astype(BF16)
    return upper, (matrix - upper.astype(F32)).astype(BF16)


def relay(
    ids_ref,
    table_ref,
    gain_ref,
    arriving,
    returning,
    stashed,
    seed_grad,
    expand,
    compress,
    w_query,
    key_weight,
    value_weight,
    w_out,
    fwd_ref,
    bwd_ref,
    expand_v,
    compress_v,
    query_v,
    kv_v,
    out_v,
    qkv_f,
    out_f,
    gram,
    basis,
    coef,
    grad_in,
    mixed_s,
    scale_s,
    qhat_s,
    rq_s,
    khat_s,
    rk_s,
    vals_s,
    probs_s,
    wide_s,
    gkv_acc,
    gcat,
    part,
    own,
    rs_in,
    e_part,
    e_in1,
    e_sum,
    e_in2,
    ld_sem,
    rs_send,
    rs_recv,
    ag_send,
    ag_recv,
    e1_send,
    e1_recv,
    e2_send,
    e2_recv,
    e3_send,
    e3_recv,
    *,
    segments,
    head_groups,
    table_rows,
):
    seg = lax.axis_index("segment")
    me = lax.axis_index("head")
    last = segments - 1
    ticks, span = ids_ref.shape
    share = span // head_groups
    width = expand_v.shape[1]
    heads = query_v.shape[1] // HEAD_SIZE
    nq = heads * HEAD_SIZE
    kv_group = QUERY_HEADS // KEY_VALUE_HEADS
    first_kv = me * heads // kv_group
    kv_cols = pl.ds(pl.multiple_of(first_kv * HEAD_SIZE, HEAD_SIZE), HEAD_SIZE)
    inv = 1.0 / math.sqrt(HEAD_SIZE)
    own_rows = pl.ds(pl.multiple_of(me * share, share), share)

    def rows_of(head):
        return pl.ds(pl.multiple_of(head * share, share), share)

    def peer(off):
        return lax.rem(me + off, head_groups)

    qchunk = min(256, nq)
    pieces = nq // qchunk
    loads = [
        (expand.at[0], expand_v),
        *[
            (
                w_query.at[0, :, i * qchunk : (i + 1) * qchunk],
                query_v.at[:, i * qchunk : (i + 1) * qchunk],
            )
            for i in range(pieces)
        ],
        (key_weight.at[0, :, kv_cols], kv_v.at[:, :HEAD_SIZE]),
        (value_weight.at[0, :, kv_cols], kv_v.at[:, HEAD_SIZE:]),
        (stashed.at[0], coef.at[ticks : 2 * ticks]),
        (compress.at[0], compress_v),
        *[
            (
                w_out.at[0, i * qchunk : (i + 1) * qchunk, :],
                out_v.at[i * qchunk : (i + 1) * qchunk, :],
            )
            for i in range(pieces)
        ],
    ]
    loads = [
        pltpu.make_async_copy(src, dst, ld_sem.at[i]) for i, (src, dst) in enumerate(loads)
    ]
    fixed = len(loads)
    arr_copy = pltpu.make_async_copy(arriving.at[0], coef.at[0], ld_sem.at[fixed])
    ret_copy = pltpu.make_async_copy(returning.at[0], grad_in.at[0], ld_sem.at[fixed + 1])
    seed_copy = pltpu.make_async_copy(seed_grad, grad_in, ld_sem.at[fixed + 1])
    for one in loads:
        one.start()

    @pl.when(seg > 0)
    def _():
        arr_copy.start()

    @pl.when(seg < last)
    def _():
        ret_copy.start()

    @pl.when(seg == last)
    def _():
        seed_copy.start()

    barrier = pltpu.get_barrier_semaphore()
    total = segments * head_groups
    mine = seg * head_groups + me
    for off in range(1, total):
        other = lax.rem(mine + off, total)
        pl.semaphore_signal(
            barrier,
            inc=1,
            device_id={
                "segment": other // head_groups,
                "head": lax.rem(other, head_groups),
            },
            device_id_type=MESH,
        )

    base = mine * table_rows
    for t in range(ticks):
        wanted = ids_ref[t : t + 1, :] - base
        places = lax.broadcasted_iota(jnp.int32, (table_ref.shape[0], span), 0)
        hot = jnp.where(places == wanted, 1.0, 0.0).astype(BF16)
        e_part[t] = mm_down(hot, table_ref[...]).astype(BF16)
    pl.semaphore_wait(barrier, total - 1)

    def e1_copy(t, slot):
        return pltpu.make_async_remote_copy(
            src_ref=e_part.at[t],
            dst_ref=e_in1.at[slot, t],
            send_sem=e1_send.at[t],
            recv_sem=e1_recv.at[slot, t],
            device_id={"segment": 0, "head": me},
            device_id_type=MESH,
        )

    @pl.when(seg > 0)
    def _():
        for t in range(ticks):
            e1_copy(t, seg).start()

    def e2_copy(t, off):
        return pltpu.make_async_remote_copy(
            src_ref=e_sum.at[t, rows_of(peer(off))],
            dst_ref=e_in2.at[t, off],
            send_sem=e2_send.at[t, off],
            recv_sem=e2_recv.at[t, off],
            device_id={"segment": seg, "head": peer(off)},
            device_id_type=MESH,
        )

    def e3_copy(t, off):
        return pltpu.make_async_remote_copy(
            src_ref=coef.at[t, own_rows],
            dst_ref=coef.at[t, own_rows],
            send_sem=e3_send.at[t, off],
            recv_sem=e3_recv.at[t, off],
            device_id={"segment": seg, "head": peer(off)},
            device_id_type=MESH,
        )

    def embed_sum(t):
        total_rows = e_part[t].astype(F32)
        for other in range(1, segments):
            e1_copy(t, other).wait_recv()
            total_rows = total_rows + e_in1[other, t].astype(F32)
        e_sum[t] = total_rows.astype(BF16)
        for off in range(1, head_groups):
            e2_copy(t, off).start()

    def embed_share(t):
        rows = e_sum[t, own_rows].astype(F32)
        for off in range(1, head_groups):
            e2_copy(t, off).wait_recv()
            rows = rows + e_in2[t, off].astype(F32)
        coef[t, own_rows] = rows.astype(BF16)
        for off in range(1, head_groups):
            e3_copy(t, off).start()

    def rs_copy(way, t, off):
        return pltpu.make_async_remote_copy(
            src_ref=part.at[way, t, rows_of(peer(off))],
            dst_ref=rs_in.at[way, t, off],
            send_sem=rs_send.at[way, t, off],
            recv_sem=rs_recv.at[way, t, off],
            device_id={"segment": seg, "head": peer(off)},
            device_id_type=MESH,
        )

    def ag_copy(way, t, from_head, to_head):
        target = coef if way == 0 else grad_in
        return pltpu.make_async_remote_copy(
            src_ref=own.at[way, t],
            dst_ref=target.at[t + 1, rows_of(from_head)],
            send_sem=ag_send.at[way, t, to_head],
            recv_sem=ag_recv.at[way, t, from_head],
            device_id={"segment": seg + (1 if way == 0 else -1), "head": to_head},
            device_id_type=MESH,
        )

    def summed(way, t):
        rows = part[way, t, own_rows].astype(F32)
        for off in range(1, head_groups):
            rs_copy(way, t, off).wait_recv()
            rows = rows + rs_in[way, t, off].astype(F32)
        return rows

    def pass_on(way, t):
        for to_head in range(head_groups):
            ag_copy(way, t, me, to_head).start()

    def replay_index(t):
        source = t - 2 * (last - seg)
        return jnp.where(source >= 0, source, ticks + t)

    def state_slot(t):
        return jnp.where(seg == last, 2 + lax.rem(t, 2), lax.rem(t, 2))

    causal = lax.broadcasted_iota(jnp.int32, (span, span), 1) <= lax.broadcasted_iota(
        jnp.int32, (span, span), 0
    )

    def section(index, slot, with_out):
        c = coef[index]
        wide = c.astype(F32)
        mixed = mm(c, gram[0]) + mm(c, gram[1])
        scaling = lax.rsqrt(jnp.sum(mixed * wide, axis=-1, keepdims=True) / width + EPS)
        mixed_s[slot] = mixed
        scale_s[slot] = scaling
        kv = mm(c, qkv_f[:, nq:]) * scaling
        keys = kv[:, :HEAD_SIZE]
        rk = lax.rsqrt(jnp.mean(keys * keys, axis=-1, keepdims=True) + EPS)
        khat = (keys * rk).astype(BF16)
        values = kv[:, HEAD_SIZE:].astype(BF16)
        khat_s[slot] = khat
        rk_s[slot] = rk
        vals_s[slot] = values

        def pair(i, carry):
            cols = pl.ds(pl.multiple_of(i * 2 * HEAD_SIZE, 2 * HEAD_SIZE), 2 * HEAD_SIZE)
            both = mm(coef[index], qkv_f[:, cols]) * scale_s[slot]
            outs = []
            for e in range(2):
                h = 2 * i + e
                q = both[:, e * HEAD_SIZE : (e + 1) * HEAD_SIZE]
                rq = lax.rsqrt(jnp.mean(q * q, axis=-1, keepdims=True) + EPS)
                qhat = (q * rq).astype(BF16)
                qhat_s[slot, h] = qhat
                rq_s[slot, h] = rq
                raw = mm_back(qhat, khat_s[slot]) * inv
                weights = jnp.where(causal, jnp.exp(raw), 0.0)
                low = (weights * (1.0 / jnp.sum(weights, axis=-1, keepdims=True))).astype(BF16)
                probs_s[slot, h] = low
                if with_out:
                    outs.append(mm(low, vals_s[slot]).astype(BF16))
            if with_out:
                wide_s[:, cols] = jnp.concatenate(outs, axis=1)
            return carry

        lax.fori_loop(0, heads // 2, pair, 0)

    def forward(t):
        section(t, 2 + lax.rem(t, 2), True)
        part[0, t] = mm(wide_s[...], out_f[...]).astype(BF16)
        for off in range(1, head_groups):
            rs_copy(0, t, off).start()

    def finish_forward(t):
        c = coef[t, own_rows]
        rows = summed(0, t) + (mm(c, basis[0]) + mm(c, basis[1]))
        rows = rows.astype(BF16)
        own[0, t] = rows
        fwd_ref[0, t] = rows

        @pl.when(jnp.logical_and(seg < last, t + 1 < ticks))
        def _():
            pass_on(0, t)

    def backward(t):
        slot = state_slot(t)
        wide_s[...] = mm_back(grad_in[t], out_f[...]).astype(BF16)
        gkv_acc[...] = jnp.zeros_like(gkv_acc)

        def pair(i, carry):
            cols = pl.ds(pl.multiple_of(i * 2 * HEAD_SIZE, 2 * HEAD_SIZE), 2 * HEAD_SIZE)
            both = wide_s[:, cols]
            outs = []
            for e in range(2):
                h = 2 * i + e
                ga = both[:, e * HEAD_SIZE : (e + 1) * HEAD_SIZE]
                low = probs_s[slot, h]
                probs = low.astype(F32)
                gp = mm_back(ga, vals_s[slot])
                inner = jnp.sum(gp * probs, axis=-1, keepdims=True)
                gs = (probs * ((gp - inner) * inv)).astype(BF16)
                qhat = qhat_s[slot, h]
                gqh = mm(gs, khat_s[slot])
                gkv_acc[0] += mm_down(gs, qhat)
                gkv_acc[1] += mm_down(low, ga)
                qw = qhat.astype(F32)
                along = jnp.mean(gqh * qw, axis=-1, keepdims=True)
                outs.append((rq_s[slot, h] * (gqh - qw * along)).astype(BF16))
            gcat[:, cols] = jnp.concatenate(outs, axis=1)
            return carry

        lax.fori_loop(0, heads // 2, pair, 0)
        gkh = gkv_acc[0]
        kw = khat_s[slot].astype(F32)
        along = jnp.mean(gkh * kw, axis=-1, keepdims=True)
        gcat[:, nq : nq + HEAD_SIZE] = (rk_s[slot] * (gkh - kw * along)).astype(BF16)
        gcat[:, nq + HEAD_SIZE :] = gkv_acc[1].astype(BF16)
        part[1, t] = mm_back(gcat[...], qkv_f[...]).astype(BF16)
        for off in range(1, head_groups):
            rs_copy(1, t, off).start()

    def finish_backward(t):
        slot = state_slot(t)
        c = coef[replay_index(t), own_rows].astype(F32)
        g = grad_in[t, own_rows]
        scaling = scale_s[slot, own_rows]
        pulled = summed(1, t)
        along = jnp.sum(pulled * c, axis=-1, keepdims=True) / width
        direct = mm_back(g, basis[0]) + mm_back(g, basis[1])
        rows = (
            scaling * pulled
            - mixed_s[slot, own_rows] * (scaling * scaling * scaling * along)
            + direct
        ).astype(BF16)
        own[1, t] = rows
        bwd_ref[0, t] = rows

        @pl.when(jnp.logical_and(seg > 0, t + 1 < ticks))
        def _():
            pass_on(1, t)

    loads[0].wait()
    gained = (expand_v[...].astype(F32) * gain_ref[...]).astype(BF16)
    up, low = halves(mm_back(expand_v[...], expand_v[...]))
    gram[0] = up
    gram[1] = low
    for i in range(pieces):
        loads[1 + i].wait()
        cols = slice(i * qchunk, (i + 1) * qchunk)
        qkv_f[:, cols] = mm(gained, query_v[:, cols]).astype(BF16)
    loads[1 + pieces].wait()
    loads[2 + pieces].wait()
    qkv_f[:, nq:] = mm(gained, kv_v[...]).astype(BF16)
    loads[3 + pieces].wait()
    loads[4 + pieces].wait()
    up, low = halves(mm(expand_v[...], compress_v[...]))
    basis[0] = up
    basis[1] = low
    for i in range(pieces):
        loads[5 + pieces + i].wait()
        rows = slice(i * qchunk, (i + 1) * qchunk)
        out_f[rows] = mm(out_v[rows, :], compress_v[...]).astype(BF16)

    @pl.when(seg > 0)
    def _():
        arr_copy.wait()

    @pl.when(seg < last)
    def _():
        ret_copy.wait()

    @pl.when(seg == last)
    def _():
        seed_copy.wait()

    @pl.when(seg == 0)
    def _():
        embed_sum(0)

    def replay_section(t):
        section(replay_index(t), lax.rem(t, 2), False)

    @pl.when(seg < last)
    def _():
        replay_section(0)

    @pl.when(seg == 0)
    def _():
        embed_share(0)

    def tick(t, carry):
        more = t + 1 < ticks

        @pl.when(seg == 0)
        def _():
            for off in range(1, head_groups):
                theirs = lax.rem(me + head_groups - off, head_groups)
                pltpu.make_async_remote_copy(
                    src_ref=coef.at[t, rows_of(theirs)],
                    dst_ref=coef.at[t, rows_of(theirs)],
                    send_sem=e3_send.at[t, off],
                    recv_sem=e3_recv.at[t, off],
                    device_id={"segment": seg, "head": peer(off)},
                    device_id_type=MESH,
                ).wait_recv()

        @pl.when(jnp.logical_and(seg > 0, t > 0))
        def _():
            for from_head in range(head_groups):
                ag_copy(0, t - 1, from_head, from_head).wait_recv()

        forward(t)

        @pl.when(t > 0)
        def _():
            finish_backward(t - 1)

        @pl.when(jnp.logical_and(seg == 0, more))
        def _():
            embed_sum(t + 1)

        @pl.when(jnp.logical_and(seg < last, more))
        def _():
            replay_section(t + 1)

        @pl.when(jnp.logical_and(seg == 0, more))
        def _():
            embed_share(t + 1)

        finish_forward(t)

        @pl.when(jnp.logical_and(seg < last, t > 0))
        def _():
            for from_head in range(head_groups):
                ag_copy(1, t - 1, from_head, from_head).wait_recv()

        backward(t)
        return carry

    lax.fori_loop(0, ticks, tick, 0)
    finish_backward(ticks - 1)

    def drain(t, carry):
        for off in range(1, head_groups):
            rs_copy(0, t, off).wait_send()
            rs_copy(1, t, off).wait_send()

        @pl.when(seg > 0)
        def _():
            e1_copy(t, seg).wait_send()

        @pl.when(seg == 0)
        def _():
            for off in range(1, head_groups):
                e2_copy(t, off).wait_send()
                e3_copy(t, off).wait_send()

        @pl.when(jnp.logical_and(seg < last, t + 1 < ticks))
        def _():
            for to_head in range(head_groups):
                ag_copy(0, t, me, to_head).wait_send()

        @pl.when(jnp.logical_and(seg > 0, t + 1 < ticks))
        def _():
            for to_head in range(head_groups):
                ag_copy(1, t, me, to_head).wait_send()

        return carry

    lax.fori_loop(0, ticks, drain, 0)


def shards(
    token_ids,
    embed_table,
    arriving,
    returning,
    stashed,
    seed_grad,
    expand,
    compress,
    norm_gain,
    w_query,
    key_weight,
    value_weight,
    w_out,
):
    segments = lax.axis_size("segment")
    head_groups = lax.axis_size("head")
    ticks, span = token_ids.shape
    rank = embed_table.shape[1]
    width = expand.shape[2]
    nq = w_query.shape[2]
    heads = nq // HEAD_SIZE
    share = span // head_groups
    table_rows = embed_table.shape[0]
    padded = -(-table_rows // 128) * 128
    table = jnp.pad(embed_table, ((0, padded - table_rows), (0, 0)))
    vmem = pl.BlockSpec(memory_space=pltpu.VMEM)
    hbm = pl.BlockSpec(memory_space=pl.ANY)
    V = pltpu.VMEM
    D = pltpu.SemaphoreType.DMA
    pieces = nq // min(256, nq)
    all_cols = nq + 2 * HEAD_SIZE
    slots = 4
    out = jax.ShapeDtypeStruct((1, ticks, share, rank), BF16)
    return pl.pallas_call(
        functools.partial(
            relay, segments=segments, head_groups=head_groups, table_rows=table_rows
        ),
        out_shape=(out, out),
        in_specs=[vmem] * 3 + [hbm] * 10,
        out_specs=(vmem, vmem),
        scratch_shapes=[
            V((rank, width), BF16),
            V((width, rank), BF16),
            V((width, nq), BF16),
            V((width, 2 * HEAD_SIZE), BF16),
            V((nq, width), BF16),
            V((rank, all_cols), BF16),
            V((nq, rank), BF16),
            V((2, rank, rank), BF16),
            V((2, rank, rank), BF16),
            V((2 * ticks, span, rank), BF16),
            V((ticks, span, rank), BF16),
            V((slots, span, rank), F32),
            V((slots, span, 1), F32),
            V((slots, heads, span, HEAD_SIZE), BF16),
            V((slots, heads, span, 1), F32),
            V((slots, span, HEAD_SIZE), BF16),
            V((slots, span, 1), F32),
            V((slots, span, HEAD_SIZE), BF16),
            V((slots, heads, span, span), BF16),
            V((span, nq), BF16),
            V((2, span, HEAD_SIZE), F32),
            V((span, all_cols), BF16),
            V((2, ticks, span, rank), BF16),
            V((2, ticks, share, rank), BF16),
            V((2, ticks, head_groups, share, rank), BF16),
            V((ticks, span, rank), BF16),
            V((segments, ticks, span, rank), BF16),
            V((ticks, span, rank), BF16),
            V((ticks, head_groups, share, rank), BF16),
            D((7 + 2 * pieces,)),
            D((2, ticks, head_groups)),
            D((2, ticks, head_groups)),
            D((2, ticks, head_groups)),
            D((2, ticks, head_groups)),
            D((ticks,)),
            D((segments, ticks)),
            D((ticks, head_groups)),
            D((ticks, head_groups)),
            D((ticks, head_groups)),
            D((ticks, head_groups)),
        ],
        compiler_params=pltpu.CompilerParams(
            collective_id=0, has_side_effects=True, vmem_limit_bytes=62 << 20
        ),
        name="relay",
    )(
        token_ids,
        table,
        norm_gain,
        arriving,
        returning,
        stashed,
        seed_grad,
        expand,
        compress,
        w_query,
        key_weight,
        value_weight,
        w_out,
    )


def solution(mesh):
    return jax.shard_map(
        shards,
        mesh=mesh,
        in_specs=(
            P("groups", None),
            P(("segment", "head"), None),
            P(("groups", "segment"), None, None),
            P(("groups", "segment"), None, None),
            P(("groups", "segment"), None, None, None),
            P("groups", None, None),
            P("segment", None, None),
            P("segment", None, None),
            P("segment", None),
            P("segment", None, "head"),
            P("segment", None, None),
            P("segment", None, None),
            P("segment", "head", None),
        ),
        out_specs=(
            P(("groups", "segment"), None, "head", None),
            P(("groups", "segment"), None, "head", None),
        ),
        check_vma=False,
    )
```

time: 463 us -> 83.3 us (0.18); the launches traced: 455 us -> 83.1 us
  matrix products: 156 us -> 0 us
  blocking collectives: 133 us -> 0 us
  Pallas kernels: 0 us -> 77.4 us
  waiting for transfers between devices: 68.8 us -> 0 us
  other arithmetic: 47.6 us -> 0 us
  local copies, waits for them, and re-layouts: 27.6 us -> 5.04 us
  between operations: 15.2 us -> 0.64 us
  starting transfers between devices: 6.22 us -> 0 us
    dot_general x62 -> x0, matrix products: 156 us -> none  [the longest x15 51.8 us: narrow_back(): lax.dot_general(former, latter, (((1,), (1,)), ((), ())), preferred_eleme...]
    psum x1 -> x0, blocking collectives: 78 us -> none  [shards(): embedded = lax.psum(picked, ('segment', 'head')).astype(jnp.bfloat16)]
    pallas_call x0 -> x1, Pallas kernels: none -> 77.4 us  [shards(): pl.pallas_call(functools.partial(relay, segments=segments, head_groups=he...]
    reduce_scatter x6 -> x0, waiting for transfers between devices: 68.1 us -> none  [the longest x3 46.5 us: shards(): lax.psum_scatter(partial_back.astype(jnp.bfloat16), 'head', scatter_dimen...]
    all_gather x4 -> x0, blocking collectives: 55.2 us -> none  [the longest x2 28.1 us: shards(): forward_recv = lax.all_gather(arrived, 'head', axis=0, tiled=True)]
    another operation x5 -> x0, other arithmetic: 13.8 us -> none
    convert_element_type x10 -> x0, other arithmetic: 13 us -> none  [the longest x3 5.25 us: section_backward(): norm_back(queries, grad_qhat).reshape(row_count, -1).astype(jnp.bfloat16)]
    another operation x3 -> x0, local copies, waits for them, and re-layouts: 8.1 us -> none
  transfers between devices with their start and end apart: 10 -> 0, of which waited for: 7 -> 0; matrix products, arithmetic and copies ran while one was open for 11% -> 0% of each run, Pallas kernels for 0% -> 0%
where the time goes in v1:
time: 83.3 us; the launch traced here: 83.1 us
  Pallas kernels  77.4 us (93%)
  local copies, waits for them, and re-layouts  5.04 us (6%)
    pallas_call x1, Pallas kernels, shards(): pl.pallas_call(functools.partial(relay, segments=segments, head_groups=he...  77.4 us
    unnamed x2, local copies, waits for them, and re-layouts  3.08 us
    pad x1, local copies, waits for them, and re-layouts, shards(): table = jnp.pad(embed_table, ((0, padded - table_rows), (0, 0)))  1.96 us

profile of v1, /device:TPU:0, one launch (start us, length us, event | category | flops | bytes accessed | tf_op | source)
XLA Modules:
  0.0 83.1 jit_solution(8687929324275075222)
XLA Ops:
  0.6 2.0 %pad.4.table_ref = bf16[1280,256]{1,0:T(8,128)(2,1)} pad(bf16[1187,256]{1,0:T(8,128)(2,1)} %param.14, bf16[]{:T(256)} %constant.2.clone.1), padding=0_93x0_0 | pad | bytes 1263106 | tf_op jit(solution)/shard_map/jit(_pad)/pad | solution.py:551
  2.6 77.4 %relay.1 = (bf16[1,3,64,256]{3,2,1,0:T(8,128)(2,1)}, bf16[1,3,64,256]{3,2,1,0:T(8,128)(2,1)}) custom-call(s32[3,256]{1,0:T(4,128)} %ids_ref.1, bf16[1280,256]{1,0:T(8,128)(2,1)} %pad.4.table_ref, f32[1,2048]{1,0:T(1,128)} %gain_ref.1, bf16[1,256,256]{2,1,0:T(8,128)(2,1)} %arriving.1, bf16[1,256,256]{2,1,0:T(8,128)(2,1)} %returning.1, ...), custom_call_target="tpu_custom_call" | custom-call | tf_op jit(solution)/shard_map/relay/pallas_call | solution.py:560
  80.0 1.5 %copy.17 = bf16[1,3,64,256]{3,2,1,0:T(8,128)(2,1)} copy(bf16[1,3,64,256]{3,2,1,0:T(8,128)(2,1)} %get-tuple-element.4) | data formatting | bytes 196608
  81.5 1.5 %copy.18 = bf16[1,3,64,256]{3,2,1,0:T(8,128)(2,1)} copy(bf16[1,3,64,256]{3,2,1,0:T(8,128)(2,1)} %get-tuple-element.5) | data formatting | bytes 196608

commit v2 on v1

--- a/solution.py
+++ b/solution.py
@@ -79,6 +79,7 @@
     e_in1,
     e_sum,
     e_in2,
+    tail,
     ld_sem,
     rs_send,
     rs_recv,
@@ -176,11 +177,28 @@
         )
 
     base = mine * table_rows
-    for t in range(ticks):
+    main = table_rows // HEAD_SIZE * HEAD_SIZE
+    rest = table_rows - main
+    even = rest // 16 * 16
+    tail[...] = jnp.zeros_like(tail)
+    if even:
+        tail[:even] = table_ref[main : main + even, :]
+    if rest > even:
+        tail[even:rest] = table_ref[main + even : table_rows, :]
+
+    def pick(t):
         wanted = ids_ref[t : t + 1, :] - base
-        places = lax.broadcasted_iota(jnp.int32, (table_ref.shape[0], span), 0)
-        hot = jnp.where(places == wanted, 1.0, 0.0).astype(BF16)
-        e_part[t] = mm_down(hot, table_ref[...]).astype(BF16)
+
+        def hot(start, count):
+            places = lax.broadcasted_iota(jnp.int32, (count, span), 0) + start
+            return jnp.where(places == wanted, 1.0, 0.0).astype(BF16)
+
+        rows = mm_down(hot(main, HEAD_SIZE), tail[...])
+        if main:
+            rows = rows + mm_down(hot(0, main), table_ref[:main, :])
+        e_part[t] = rows.astype(BF16)
+
+    pick(0)
     pl.semaphore_wait(barrier, total - 1)
 
     def e1_copy(t, slot):
@@ -195,8 +213,10 @@
 
     @pl.when(seg > 0)
     def _():
-        for t in range(ticks):
-            e1_copy(t, seg).start()
+        e1_copy(0, seg).start()
+
+    for t in range(1, ticks):
+        pick(t)
 
     def e2_copy(t, off):
         return pltpu.make_async_remote_copy(
@@ -275,9 +295,17 @@
     def state_slot(t):
         return jnp.where(seg == last, 2 + lax.rem(t, 2), lax.rem(t, 2))
 
-    causal = lax.broadcasted_iota(jnp.int32, (span, span), 1) <= lax.broadcasted_iota(
-        jnp.int32, (span, span), 0
-    )
+    half = span // 2
+
+    def pair_cols(i):
+        return pl.ds(pl.multiple_of(i * 2 * HEAD_SIZE, 2 * HEAD_SIZE), 2 * HEAD_SIZE)
+
+    causal = []
+    for rb in range(2):
+        shape = (half, (rb + 1) * half)
+        row = lax.broadcasted_iota(jnp.int32, shape, 0) + rb * half
+        row = jnp.concatenate([row, row], axis=0)
+        causal.append(lax.broadcasted_iota(jnp.int32, row.shape, 1) <= row)
 
     def section(index, slot, with_out):
         c = coef[index]
@@ -296,24 +324,28 @@
         vals_s[slot] = values
 
         def pair(i, carry):
-            cols = pl.ds(pl.multiple_of(i * 2 * HEAD_SIZE, 2 * HEAD_SIZE), 2 * HEAD_SIZE)
+            cols = pair_cols(i)
             both = mm(coef[index], qkv_f[:, cols]) * scale_s[slot]
-            outs = []
+            hats = []
+            scales = []
             for e in range(2):
-                h = 2 * i + e
                 q = both[:, e * HEAD_SIZE : (e + 1) * HEAD_SIZE]
                 rq = lax.rsqrt(jnp.mean(q * q, axis=-1, keepdims=True) + EPS)
-                qhat = (q * rq).astype(BF16)
-                qhat_s[slot, h] = qhat
-                rq_s[slot, h] = rq
-                raw = mm_back(qhat, khat_s[slot]) * inv
-                weights = jnp.where(causal, jnp.exp(raw), 0.0)
+                hats.append((q * rq).astype(BF16))
+                scales.append(rq)
+            for rb in range(2):
+                rows = slice(rb * half, (rb + 1) * half)
+                known = (rb + 1) * half
+                qq = jnp.concatenate([x[rows] for x in hats], axis=0)
+                qhat_s[slot, i, rb] = qq
+                rq_s[slot, i, rb] = jnp.concatenate([x[rows] for x in scales], axis=0)
+                raw = mm_back(qq, khat_s[slot, :known]) * inv
+                weights = jnp.where(causal[rb], jnp.exp(raw), 0.0)
                 low = (weights * (1.0 / jnp.sum(weights, axis=-1, keepdims=True))).astype(BF16)
-                probs_s[slot, h] = low
+                probs_s[slot, i, rb, :, :known] = low
                 if with_out:
-                    outs.append(mm(low, vals_s[slot]).astype(BF16))
-            if with_out:
-                wide_s[:, cols] = jnp.concatenate(outs, axis=1)
+                    att = mm(low, vals_s[slot, :known]).astype(BF16)
+                    wide_s[rows, cols] = jnp.concatenate([att[:half], att[half:]], axis=1)
             return carry
 
         lax.fori_loop(0, heads // 2, pair, 0)
@@ -341,25 +373,25 @@
         gkv_acc[...] = jnp.zeros_like(gkv_acc)
 
         def pair(i, carry):
-            cols = pl.ds(pl.multiple_of(i * 2 * HEAD_SIZE, 2 * HEAD_SIZE), 2 * HEAD_SIZE)
-            both = wide_s[:, cols]
-            outs = []
-            for e in range(2):
-                h = 2 * i + e
-                ga = both[:, e * HEAD_SIZE : (e + 1) * HEAD_SIZE]
-                low = probs_s[slot, h]
+            cols = pair_cols(i)
+            for rb in range(2):
+                rows = slice(rb * half, (rb + 1) * half)
+                known = (rb + 1) * half
+                both = wide_s[rows, cols]
+                ga = jnp.concatenate([both[:, :HEAD_SIZE], both[:, HEAD_SIZE:]], axis=0)
+                low = probs_s[slot, i, rb, :, :known]
                 probs = low.astype(F32)
-                gp = mm_back(ga, vals_s[slot])
+                gp = mm_back(ga, vals_s[slot, :known])
                 inner = jnp.sum(gp * probs, axis=-1, keepdims=True)
                 gs = (probs * ((gp - inner) * inv)).astype(BF16)
-                qhat = qhat_s[slot, h]
-                gqh = mm(gs, khat_s[slot])
-                gkv_acc[0] += mm_down(gs, qhat)
-                gkv_acc[1] += mm_down(low, ga)
+                qhat = qhat_s[slot, i, rb]
+                gqh = mm(gs, khat_s[slot, :known])
+                gkv_acc[0, :known] += mm_down(gs, qhat)
+                gkv_acc[1, :known] += mm_down(low, ga)
                 qw = qhat.astype(F32)
                 along = jnp.mean(gqh * qw, axis=-1, keepdims=True)
-                outs.append((rq_s[slot, h] * (gqh - qw * along)).astype(BF16))
-            gcat[:, cols] = jnp.concatenate(outs, axis=1)
+                gq = (rq_s[slot, i, rb] * (gqh - qw * along)).astype(BF16)
+                gcat[rows, cols] = jnp.concatenate([gq[:half], gq[half:]], axis=1)
             return carry
 
         lax.fori_loop(0, heads // 2, pair, 0)
@@ -404,6 +436,11 @@
     loads[1 + pieces].wait()
     loads[2 + pieces].wait()
     qkv_f[:, nq:] = mm(gained, kv_v[...]).astype(BF16)
+
+    @pl.when(seg == 0)
+    def _():
+        embed_sum(0)
+
     loads[3 + pieces].wait()
     loads[4 + pieces].wait()
     up, low = halves(mm(expand_v[...], compress_v[...]))
@@ -426,20 +463,20 @@
     def _():
         seed_copy.wait()
 
-    @pl.when(seg == 0)
-    def _():
-        embed_sum(0)
-
     def replay_section(t):
         section(replay_index(t), lax.rem(t, 2), False)
 
-    @pl.when(seg < last)
-    def _():
-        replay_section(0)
-
     @pl.when(seg == 0)
     def _():
         embed_share(0)
+
+    ahead = jnp.where(seg == last, 0, jnp.where(seg == 0, min(2, ticks), 1))
+
+    def early(t, carry):
+        replay_section(t)
+        return carry
+
+    lax.fori_loop(0, ahead, early, 0)
 
     def tick(t, carry):
         more = t + 1 < ticks
@@ -462,6 +499,10 @@
             for from_head in range(head_groups):
                 ag_copy(0, t - 1, from_head, from_head).wait_recv()
 
+        @pl.when(jnp.logical_and(seg > 0, more))
+        def _():
+            e1_copy(t + 1, seg).start()
+
         forward(t)
 
         @pl.when(t > 0)
@@ -472,7 +513,7 @@
         def _():
             embed_sum(t + 1)
 
-        @pl.when(jnp.logical_and(seg < last, more))
+        @pl.when(jnp.logical_and(t + 1 >= ahead, jnp.logical_and(seg < last, more)))
         def _():
             replay_section(t + 1)
 
@@ -547,8 +588,6 @@
     heads = nq // HEAD_SIZE
     share = span // head_groups
     table_rows = embed_table.shape[0]
-    padded = -(-table_rows // 128) * 128
-    table = jnp.pad(embed_table, ((0, padded - table_rows), (0, 0)))
     vmem = pl.BlockSpec(memory_space=pltpu.VMEM)
     hbm = pl.BlockSpec(memory_space=pl.ANY)
     V = pltpu.VMEM
@@ -578,12 +617,12 @@
             V((ticks, span, rank), BF16),
             V((slots, span, rank), F32),
             V((slots, span, 1), F32),
-            V((slots, heads, span, HEAD_SIZE), BF16),
-            V((slots, heads, span, 1), F32),
+            V((slots, heads // 2, 2, span, HEAD_SIZE), BF16),
+            V((slots, heads // 2, 2, span, 1), F32),
             V((slots, span, HEAD_SIZE), BF16),
             V((slots, span, 1), F32),
             V((slots, span, HEAD_SIZE), BF16),
-            V((slots, heads, span, span), BF16),
+            V((slots, heads // 2, 2, span, span), BF16),
             V((span, nq), BF16),
             V((2, span, HEAD_SIZE), F32),
             V((span, all_cols), BF16),
@@ -594,6 +633,7 @@
             V((segments, ticks, span, rank), BF16),
             V((ticks, span, rank), BF16),
             V((ticks, head_groups, share, rank), BF16),
+            V((HEAD_SIZE, rank), BF16),
             D((7 + 2 * pieces,)),
             D((2, ticks, head_groups)),
             D((2, ticks, head_groups)),
@@ -612,7 +652,7 @@
         name="relay",
     )(
         token_ids,
-        table,
+        embed_table,
         norm_gain,
         arriving,
         returning,

time: 83.3 us -> 78.8 us (0.946)
  Pallas kernels: 77.4 us -> 74.8 us
  local copies, waits for them, and re-layouts: 5.04 us -> 3.08 us
    pallas_call x1, Pallas kernels: 77.4 us -> 74.8 us  [shards(): pl.pallas_call(functools.partial(relay, segments=segments, head_groups=he...]
    pad x1 -> x0, local copies, waits for them, and re-layouts: 1.96 us -> none  [shards(): table = jnp.pad(embed_table, ((0, padded - table_rows), (0, 0)))]
where the time goes in v2:
time: 78.8 us; the launch traced here: 78.6 us
  Pallas kernels  74.8 us (95%)
  local copies, waits for them, and re-layouts  3.08 us (4%)
    pallas_call x1, Pallas kernels, shards(): pl.pallas_call(functools.partial(relay, segments=segments, head_groups=he...  74.8 us
    unnamed x2, local copies, waits for them, and re-layouts  3.08 us

profile of v2, /device:TPU:0, one launch (start us, length us, event | category | flops | bytes accessed | tf_op | source)
XLA Modules:
  0.0 78.6 jit_solution(16527835197365354394)
XLA Ops:
  0.6 74.8 %relay.1 = (bf16[1,3,64,256]{3,2,1,0:T(8,128)(2,1)}, bf16[1,3,64,256]{3,2,1,0:T(8,128)(2,1)}) custom-call(s32[3,256]{1,0:T(4,128)} %ids_ref.1, bf16[1187,256]{1,0:T(8,128)(2,1)} %table_ref.1, f32[1,2048]{1,0:T(1,128)} %gain_ref.1, bf16[1,256,256]{2,1,0:T(8,128)(2,1)} %arriving.1, bf16[1,256,256]{2,1,0:T(8,128)(2,1)} %returning.1, ...), custom_call_target="tpu_custom_call" | custom-call | tf_op jit(solution)/shard_map/relay/pallas_call | solution.py:599
  75.5 1.5 %copy.17 = bf16[1,3,64,256]{3,2,1,0:T(8,128)(2,1)} copy(bf16[1,3,64,256]{3,2,1,0:T(8,128)(2,1)} %get-tuple-element.4) | data formatting | bytes 196608
  77.0 1.5 %copy.18 = bf16[1,3,64,256]{3,2,1,0:T(8,128)(2,1)} copy(bf16[1,3,64,256]{3,2,1,0:T(8,128)(2,1)} %get-tuple-element.5) | data formatting | bytes 196608

commit v3 on v2

--- a/solution.py
+++ b/solution.py
@@ -466,14 +466,15 @@
     def replay_section(t):
         section(replay_index(t), lax.rem(t, 2), False)
 
-    @pl.when(seg == 0)
-    def _():
-        embed_share(0)
-
     ahead = jnp.where(seg == last, 0, jnp.where(seg == 0, min(2, ticks), 1))
 
     def early(t, carry):
         replay_section(t)
+
+        @pl.when(jnp.logical_and(seg == 0, t == 0))
+        def _():
+            embed_share(0)
+
         return carry
 
     lax.fori_loop(0, ahead, early, 0)

time: 78.8 us -> 79 us (level)
  no operation moved by 1% of the time
where the time goes in v3:
time: 79 us; the launch traced here: 78.8 us
  Pallas kernels  75 us (95%)
  local copies, waits for them, and re-layouts  3.08 us (4%)
    pallas_call x1, Pallas kernels, shards(): pl.pallas_call(functools.partial(relay, segments=segments, head_groups=he...  75 us
    unnamed x2, local copies, waits for them, and re-layouts  3.08 us

profile of v3, /device:TPU:0, one launch (start us, length us, event | category | flops | bytes accessed | tf_op | source)
XLA Modules:
  0.0 78.8 jit_solution(2443013244572219586)
XLA Ops:
  0.6 75.0 %relay.1 = (bf16[1,3,64,256]{3,2,1,0:T(8,128)(2,1)}, bf16[1,3,64,256]{3,2,1,0:T(8,128)(2,1)}) custom-call(s32[3,256]{1,0:T(4,128)} %ids_ref.1, bf16[1187,256]{1,0:T(8,128)(2,1)} %table_ref.1, f32[1,2048]{1,0:T(1,128)} %gain_ref.1, bf16[1,256,256]{2,1,0:T(8,128)(2,1)} %arriving.1, bf16[1,256,256]{2,1,0:T(8,128)(2,1)} %returning.1, ...), custom_call_target="tpu_custom_call" | custom-call | tf_op jit(solution)/shard_map/relay/pallas_call | solution.py:600
  75.7 1.5 %copy.17 = bf16[1,3,64,256]{3,2,1,0:T(8,128)(2,1)} copy(bf16[1,3,64,256]{3,2,1,0:T(8,128)(2,1)} %get-tuple-element.4) | data formatting | bytes 196608
  77.2 1.5 %copy.18 = bf16[1,3,64,256]{3,2,1,0:T(8,128)(2,1)} copy(bf16[1,3,64,256]{3,2,1,0:T(8,128)(2,1)} %get-tuple-element.5) | data formatting | bytes 196608
